TPU v7x, 32 devices: a whole 2x2x4 slice. The times are simulated.
32 devices in a mesh: seq: 8 (over y, x, core), sub: 4 (over z).
Axes of the slice: x: 2, y: 2, z: 4, core: 2. Of those that a mesh axis runs over, the one named last changes fastest.
Arguments:
- query_rows: bfloat16 [8192, 1120], P(('seq', 'sub')), may hold values from -6 to 6
- key_rows: bfloat16 [8192, 1120], P(('seq', 'sub')), may hold values from -6 to 6
- value_rows: bfloat16 [8192, 1120], P(('seq', 'sub')), may hold values from -6 to 6
- query_tangent: bfloat16 [8192, 1120], P(('seq', 'sub')), may hold values from -6 to 6
- key_tangent: bfloat16 [8192, 1120], P(('seq', 'sub')), may hold values from -6 to 6
- value_tangent: bfloat16 [8192, 1120], P(('seq', 'sub')), may hold values from -6 to 6
- teacher: bfloat16 [8192, 2240], P(('seq', 'sub')), may hold values from -64 to 64
- out_weight: bfloat16 [1120, 2240], replicated, may hold values from -0.1875 to 0.1875
- norm_gain: float32 [1120], replicated, may hold values from 0.1 to 1.9
- clip_length: int32 [1], replicated, may hold values from 4096 to 8192
- block_mask: int32 [128], P(('seq', 'sub')), may hold values 0 or 1
Outputs:
- residual: bfloat16 [8192, 2240], P(('seq', 'sub'))
- grad_query: bfloat16 [8192, 1120], P(('seq', 'sub'))
- grad_key: bfloat16 [8192, 1120], P(('seq', 'sub'))
- grad_value: bfloat16 [8192, 1120], P(('seq', 'sub'))
All inputs are finite; a program needn't handle non-finite values. No bound on the sum of `block_mask` on one device may be relied on, other than what follows from the above.
Results may differ from a plain program's by a relative error of at most 0.007.
Values may be sent and summed in bfloat16 or wider, within the bound.
A program may use at most 64 MiB of HBM per device.

v0:
```python
import functools

import jax
import jax.numpy as jnp
from jax import lax
from jax.experimental import pallas as pl
from jax.experimental.pallas import tpu as pltpu
from jax.sharding import PartitionSpec as P

H = 10
E = 112
BLK = 64


MESH = pl.DeviceIdType.MESH
LANES = 128
f32 = jnp.float32
bf16 = jnp.bfloat16


def norm_back(unnorm, scale_inv, weighted):
    inner_mean = jnp.mean(unnorm * weighted, axis=0, keepdims=True)
    return scale_inv * weighted - unnorm * (scale_inv * scale_inv * scale_inv) * inner_mean


def dot(left, right, over):
    return lax.dot_general(left, right, ((over[:1], over[1:]), ((), ())), preferred_element_type=f32)


class Where:
    def __init__(self, chips, depth):
        seq = lax.axis_index("seq")
        self.sub = lax.axis_index("sub")
        self.depth = depth
        self.chips = chips
        self.core = lax.rem(seq, 2)
        self.chip = (seq // 2) * depth + self.sub
        self.partner = (seq + 1 - 2 * self.core, self.sub)

    def peer(self, index):
        return (index // self.depth) * 2 + self.core, lax.rem(index, self.depth)

    def ahead(self, step):
        return lax.rem(self.chip + step, self.chips)

    def behind(self, step):
        return lax.rem(self.chip + self.chips - step, self.chips)


def greet(at):
    barrier = pltpu.get_barrier_semaphore()
    pl.semaphore_signal(barrier, inc=1, device_id=at.partner, device_id_type=MESH)

    @pl.loop(1, at.chips)
    def _(step):
        pl.semaphore_signal(
            barrier, inc=1, device_id=at.peer(at.ahead(step)), device_id_type=MESH
        )


def all_total(at, piece, wide, near, sent, out, half, mine, parts, sems, between=None, after=None):
    s0, r0, s1, r1, s2, r2, s3, r3 = sems
    core, chip, chips = at.core, at.chip, at.chips

    def copy(src, dst, send, recv, to):
        return pltpu.make_async_remote_copy(
            src_ref=src,
            dst_ref=dst,
            send_sem=send,
            recv_sem=recv,
            device_id=to,
            device_id_type=MESH,
        )

    def rows(index, side=None):
        base = index if side is None else side * chips + index
        return pl.ds(pl.multiple_of(base * piece, 16), piece)

    def scatter(index, slot):
        return copy(
            mine.at[rows(index)], parts.at[rows(slot)], s1.at[index], r1.at[slot], at.peer(index)
        )

    def gather(index, slot):
        return copy(
            out.at[rows(chip, core)],
            out.at[rows(slot, core)],
            s2.at[index],
            r2.at[slot],
            at.peer(index),
        )

    def forward(index, side):
        return copy(
            out.at[rows(index, core)],
            out.at[rows(index, side)],
            s3.at[index],
            r3.at[index],
            at.partner,
        )

    size = wide.shape[0]
    for block in range(wide.shape[1] // LANES):
        lanes = wide[:, block * LANES : (block + 1) * LANES]
        near[block * size : (block + 1) * size, :] = lanes
        sent[block * size : (block + 1) * size, :] = lanes.astype(bf16)
    used = size * (wide.shape[1] // LANES)
    if used < near.shape[0]:
        near[used:, :] = jnp.zeros((near.shape[0] - used, LANES), f32)
        sent[used:, :] = jnp.zeros((near.shape[0] - used, LANES), bf16)

    other = pl.ds(pl.multiple_of((1 - core) * (chips * piece), 16), chips * piece)
    swap = copy(sent.at[other], half, s0, r0, at.partner)
    swap.start()
    if between is not None:
        between()
    swap.wait()

    def pair(index):
        return near[rows(index, core), :] + half[rows(index), :].astype(f32)

    @pl.loop(1, chips)
    def _(step):
        index = at.ahead(step)
        mine[rows(index), :] = pair(index).astype(bf16)
        scatter(index, chip).start()

    if after is not None:
        after()

    def add(step, acc):
        index = at.behind(step)
        scatter(index, index).wait_recv()
        return acc + parts[rows(index), :].astype(f32)

    out[rows(chip, core), :] = lax.fori_loop(1, chips, add, pair(chip)).astype(bf16)

    @pl.loop(1, chips)
    def _(step):
        gather(at.ahead(step), chip).start()

    forward(chip, core).start()

    @pl.loop(1, chips)
    def _(step):
        index = at.behind(step)
        gather(index, index).wait_recv()
        forward(index, core).start()

    @pl.loop(1, chips)
    def _(step):
        index = at.ahead(step)
        scatter(index, chip).wait_send()
        gather(index, chip).wait_send()

    @pl.loop(0, chips)
    def _(step):
        index = at.behind(step)
        forward(index, 1 - core).wait_recv()
        forward(index, core).wait_send()

    for block in range(wide.shape[1] // LANES):
        wide[:, block * LANES : (block + 1) * LANES] = out[
            block * size : (block + 1) * size, :
        ].astype(f32)


def kept_tokens(tok, first, clip_ref, flags_ref):
    token = lax.broadcasted_iota(jnp.int32, (8, tok), 1)
    kept = jnp.zeros((8, tok), jnp.int32)
    for block in range(tok // BLK):
        inside = (token >= block * BLK) & (token < (block + 1) * BLK)
        kept = jnp.where(inside, flags_ref[block], kept)
    before = token + first < clip_ref[0]
    return jnp.where(before & (kept == 1), 1.0, 0.0).astype(f32)[:1]


def step_kernel(
    chips, depth, pieces,
    q_hbm, k_hbm, v_hbm, qt_hbm, kt_hbm, vt_hbm, t_hbm, w_hbm, gain_ref, clip_ref, flags_ref,
    res_hbm, gq_hbm, grad_ref,
    q, k, v, qt, kt, vt, teach, weight, loads,
    wide1, near1, sent1, out1, half1, mine1, parts1,
    wide2, near2, sent2, out2, half2, mine2, parts2,
    unnorm, scale, normed, ngrad, ugrad, turned, gain, res_ref, gq_ref, stores,
    *sems,
):
    at = Where(chips, depth)
    tok = q.shape[1]
    incoming = [
        pltpu.make_async_copy(src, dst, loads.at[i])
        for i, (src, dst) in enumerate(
            [
                (k_hbm, k),
                (v_hbm, v),
                (kt_hbm, kt),
                (vt_hbm, vt),
                (w_hbm, weight),
                (q_hbm, q),
                (qt_hbm, qt),
                (t_hbm, teach),
            ]
        )
    ]
    greet(at)
    for load in incoming:
        load.start()

    device = lax.axis_index("seq") * depth + at.sub
    valid = kept_tokens(tok, device * tok, clip_ref, flags_ref)

    def head(ref, h):
        return ref[h * E : (h + 1) * E, :]

    def square(ref, h):
        return ref[:, h * E : (h + 1) * E].astype(bf16)

    def key_parts(h):
        keys = head(k, h).astype(f32)
        slope = jnp.where(keys > 0, 1.0, 0.0) * valid
        return jnp.maximum(keys, 0.0) * valid, slope

    edge = wide1.shape[1] - LANES
    wide1[:, edge:] = jnp.zeros((wide1.shape[0], LANES), f32)
    wide2[:, edge:] = jnp.zeros((wide2.shape[0], LANES), f32)
    for load in incoming[:4]:
        load.wait()
    for h in range(H):
        feat, slope = key_parts(h)
        feat = feat.astype(bf16)
        along = (slope * head(kt, h).astype(f32)).astype(bf16)
        vals = head(v, h)
        cols = slice(h * E, (h + 1) * E)
        wide1[:E, cols] = dot(vals, feat, (1, 1))
        wide1[E:, cols] = dot(vals, along, (1, 1)) + dot(head(vt, h), feat, (1, 1))

    def prepare():
        row = lax.broadcasted_iota(jnp.int32, (E, E), 0)
        col = lax.broadcasted_iota(jnp.int32, (E, E), 1)
        for h in range(H):
            spread = jnp.where(row == col, gain_ref[:, h * E : (h + 1) * E], 0.0)
            gain[h * E : (h + 1) * E, :] = jnp.sum(spread, axis=1, keepdims=True)
        for load in incoming[4:]:
            load.wait()
        for start in range(0, weight.shape[1], 256):
            stop = min(start + 256, weight.shape[1])
            turned[start:stop, :] = weight[:, start:stop].T

    pl.semaphore_wait(pltpu.get_barrier_semaphore(), chips)
    all_total(
        at, pieces[0], wide1, near1, sent1, out1, half1, mine1, parts1, sems[:8], None, prepare
    )

    def query(h):
        rows = head(q, h).astype(f32)
        return jnp.maximum(rows, 0.0).astype(bf16), jnp.where(rows > 0, 1.0, 0.0).astype(f32)

    for h in range(H):
        rows = slice(h * E, (h + 1) * E)
        both = square(wide1, h)
        feat, slope = query(h)
        along = (slope * head(qt, h).astype(f32)).astype(bf16)
        un = dot(both[:E], feat, (1, 0))
        un_dot = dot(both[:E], along, (1, 0)) + dot(both[E:], feat, (1, 0))
        inv = lax.rsqrt(jnp.mean(un * un, axis=0, keepdims=True) + 1e-06)
        unnorm[rows, :] = un
        scale[h] = inv
        normed[rows, :] = (gain[rows, :] * norm_back(un, inv, un_dot)).astype(bf16)

    velocity = dot(turned[...], normed[...], (1, 0))
    res_ref[...] = (velocity - teach[...].astype(f32)).astype(bf16)
    res_out = pltpu.make_async_copy(res_ref, res_hbm, stores.at[0])
    gq_out = pltpu.make_async_copy(gq_ref, gq_hbm, stores.at[1])
    res_out.start()
    ngrad[...] = dot(weight[...], res_ref[...], (1, 0))
    for h in range(H):
        rows = slice(h * E, (h + 1) * E)
        weighted = gain[rows, :] * head(ngrad, h)
        grad = norm_back(head(unnorm, h), scale[h], weighted).astype(bf16)
        ugrad[rows, :] = grad
        wide2[:, h * E : (h + 1) * E] = dot(grad, query(h)[0], (1, 1))

    def query_grads():
        for h in range(H):
            back = dot(square(wide1, h)[:E], head(ugrad, h), (0, 0))
            gq_ref[h * E : (h + 1) * E, :] = (query(h)[1] * back).astype(bf16)
        gq_out.start()

    all_total(
        at, pieces[1], wide2, near2, sent2, out2, half2, mine2, parts2, sems[8:], None, query_grads
    )

    grad_ref[...] = wide2[...].astype(bf16)
    res_out.wait()
    gq_out.wait()


def finish_kernel(
    first_ref, k_hbm, v_hbm, res_hbm, gq_hbm, grad_ref, clip_ref, flags_ref,
    res_out, gq_out, gk_out, gv_out,
    k, v, res, gq, gk, gv, loads, stores,
):
    tok = k.shape[1]
    pairs = [(k_hbm, k), (v_hbm, v), (res_hbm, res), (gq_hbm, gq)]
    incoming = [pltpu.make_async_copy(*pair, loads.at[i]) for i, pair in enumerate(pairs)]
    pairs = [(res, res_out), (gq, gq_out), (gk, gk_out), (gv, gv_out)]
    outgoing = [pltpu.make_async_copy(*pair, stores.at[i]) for i, pair in enumerate(pairs)]
    for load in incoming:
        load.start()
    valid = kept_tokens(tok, first_ref[0], clip_ref, flags_ref)
    incoming[0].wait()
    incoming[1].wait()
    for h in range(H):
        rows = slice(h * E, (h + 1) * E)
        total = grad_ref[:, rows]
        keys = k[rows, :].astype(f32)
        slope = jnp.where(keys > 0, 1.0, 0.0) * valid
        feat = (jnp.maximum(keys, 0.0) * valid).astype(bf16)
        gk[rows, :] = (slope * dot(total, v[rows, :], (0, 0))).astype(bf16)
        gv[rows, :] = dot(total, feat, (1, 0)).astype(bf16)
        if h == 1:
            for load, store in zip(incoming[2:], outgoing[:2]):
                load.wait()
                store.start()
    outgoing[2].start()
    outgoing[3].start()
    for store in outgoing:
        store.wait()


def local(
    query_rows,
    key_rows,
    value_rows,
    query_tangent,
    key_tangent,
    value_tangent,
    teacher,
    out_weight,
    norm_gain,
    clip_length,
    block_mask,
):
    tok, width = query_rows.shape
    depth = lax.axis_size("sub")
    chips = lax.axis_size("seq") // 2 * depth
    padded = -(-width // LANES) * LANES
    vmem = pltpu.VMEM
    dma = pltpu.SemaphoreType.DMA
    pieces = []
    totals = []
    for size in (2 * E, E):
        piece = -(-(size * padded // LANES) // (32 * chips)) * 16
        pieces.append(piece)
        half = (chips * piece, LANES)
        full = (2 * chips * piece, LANES)
        totals += [vmem((size, padded), f32), vmem(full, f32), vmem(full, bf16), vmem(full, bf16)]
        totals += [vmem(half, bf16)] * 3
    arrays = (query_rows, key_rows, value_rows, query_tangent, key_tangent, value_tangent)
    arrays = tuple(array.T for array in arrays + (teacher,)) + (out_weight,)
    anywhere = pl.BlockSpec(memory_space=pl.ANY)
    in_vmem = pl.BlockSpec(memory_space=vmem)
    in_smem = pl.BlockSpec(memory_space=pltpu.SMEM)
    wide_t = jax.ShapeDtypeStruct((width, tok), bf16)
    res_t = jax.ShapeDtypeStruct(teacher.shape[::-1], bf16)
    res, grad_query, grad = pl.pallas_call(
        functools.partial(step_kernel, chips, depth, pieces),
        out_shape=(res_t, wide_t, jax.ShapeDtypeStruct((E, padded), bf16)),
        in_specs=[anywhere] * 8 + [in_vmem, in_smem, in_smem],
        out_specs=[anywhere, anywhere, in_vmem],
        scratch_shapes=[vmem(array.shape, array.dtype) for array in arrays]
        + [dma((8,))]
        + totals
        + [
            vmem((width, tok), f32),
            vmem((H, 1, tok), f32),
            vmem((width, tok), bf16),
            vmem((width, tok), f32),
            vmem((width, tok), bf16),
            vmem(out_weight.shape[::-1], bf16),
            vmem((width, 1), f32),
            vmem(res_t.shape, bf16),
            vmem((width, tok), bf16),
            dma((2,)),
        ]
        + ([dma, dma] + [dma((chips,))] * 6) * 2,
        compiler_params=pltpu.CompilerParams(collective_id=0, has_side_effects=True),
    )(*arrays, norm_gain[None, :], clip_length, block_mask)
    first = (lax.axis_index("seq") * depth + lax.axis_index("sub")) * tok
    outs = pl.pallas_call(
        finish_kernel,
        out_shape=(res_t, wide_t, wide_t, wide_t),
        in_specs=[in_smem] + [anywhere] * 4 + [in_vmem, in_smem, in_smem],
        out_specs=[anywhere] * 4,
        scratch_shapes=[vmem(wide_t.shape, bf16)] * 2
        + [vmem(res_t.shape, bf16)]
        + [vmem(wide_t.shape, bf16)] * 3
        + [dma((4,)), dma((4,))],
    )(first[None], arrays[1], arrays[2], res, grad_query, grad, clip_length, block_mask)
    return tuple(out.T for out in outs)


def solution(mesh):
    return jax.shard_map(
        local,
        mesh=mesh,
        in_specs=(
            P(("seq", "sub"), None),
            P(("seq", "sub"), None),
            P(("seq", "sub"), None),
            P(("seq", "sub"), None),
            P(("seq", "sub"), None),
            P(("seq", "sub"), None),
            P(("seq", "sub"), None),
            P(),
            P(),
            P(),
            P(("seq", "sub")),
        ),
        out_specs=(
            P(("seq", "sub"), None),
            P(("seq", "sub"), None),
            P(("seq", "sub"), None),
            P(("seq", "sub"), None),
        ),
        check_vma=False,
    )
```

profile of v0, /device:TPU:0, one launch (start us, length us, event | category | flops | bytes accessed | tf_op | source)
XLA Modules:
  0.0 53.4 jit_solution(9841083479865095243)
XLA Ops:
  1.3 1.3 %broadcast_in_dim.7.gain_ref = f32[1,1120]{1,0:T(1,128)} reshape(f32[1120]{0:T(1024)} %param.19) | data formatting | bytes 8960 | tf_op jit(solution)/shard_map/broadcast_in_dim | solution.py:388
  2.6 46.6 %shard_map.138 = (bf16[2240,256]{1,0:T(8,128)(2,1)}, bf16[1120,256]{1,0:T(8,128)(2,1)}, bf16[112,1152]{1,0:T(8,128)(2,1)}) custom-call(bf16[1120,256]{1,0:T(8,128)(2,1)} %bitcast.17, bf16[1120,256]{1,0:T(8,128)(2,1)} %bitcast.12, bf16[1120,256]{1,0:T(8,128)(2,1)} %bitcast.14, bf16[1120,256]{1,0:T(8,128)(2,1)} %bitcast.18, bf16[1120,256]{1,0:T(8,128)(2,1)} %bitcast.19, ...), custom_call_target="tpu_custom_call" | custom-call | tf_op jit(solution)/shard_map/pallas_call | solution.py:366
  49.2 4.3 %shard_map.139 = (bf16[2240,256]{1,0:T(8,128)(2,1)}, bf16[1120,256]{1,0:T(8,128)(2,1)}, bf16[1120,256]{1,0:T(8,128)(2,1)}, bf16[1120,256]{1,0:T(8,128)(2,1)}) custom-call(s32[1]{0:T(128)} %bitcast.first_ref, bf16[1120,256]{1,0:T(8,128)(2,1)} %bitcast.13, bf16[1120,256]{1,0:T(8,128)(2,1)} %bitcast.15, bf16[2240,256]{1,0:T(8,128)(2,1)} %get-tuple-element.11.res_hbm, ...), custom_call_target="tpu_custom_call" | custom-call | tf_op jit(solution)/shard_map/pallas_call | solution.py:390
where the time goes:
time: 53.7 us; the launch traced here: 53.4 us
  Pallas kernels  50.9 us (95%)
  local copies, waits for them, and re-layouts  1.29 us (2%)
  between operations  1.29 us (2%)
    pallas_call x1, Pallas kernels, local(): pl.pallas_call(functools.partial(step_kernel, chips, depth, pieces), out_...  46.6 us
    pallas_call x1, Pallas kernels, local(): pl.pallas_call(finish_kernel, out_shape=(res_t, wide_t, wide_t, wide_t),...  4.28 us
    broadcast_in_dim x1, local copies, waits for them, and re-layouts, local(): norm_gain[None, :]  1.29 us

commit v1 on v0

--- a/solution.py
+++ b/solution.py
@@ -14,6 +14,8 @@
 
 MESH = pl.DeviceIdType.MESH
 LANES = 128
+VMEM_BYTES = 67043328
+FINISH_VMEM = 16 << 20
 f32 = jnp.float32
 bf16 = jnp.bfloat16
 
@@ -178,11 +180,11 @@
 def step_kernel(
     chips, depth, pieces,
     q_hbm, k_hbm, v_hbm, qt_hbm, kt_hbm, vt_hbm, t_hbm, w_hbm, gain_ref, clip_ref, flags_ref,
-    res_hbm, gq_hbm, grad_ref,
-    q, k, v, qt, kt, vt, teach, weight, loads,
+    res_ref, gq_ref, grad_ref, k, v, valid_ref,
+    q, qt, kt, vt, teach, weight, loads,
     wide1, near1, sent1, out1, half1, mine1, parts1,
     wide2, near2, sent2, out2, half2, mine2, parts2,
-    unnorm, scale, normed, ngrad, ugrad, turned, gain, res_ref, gq_ref, stores,
+    unnorm, scale, normed, ngrad, ugrad, turned, gain,
     *sems,
 ):
     at = Where(chips, depth)
@@ -203,11 +205,12 @@
         )
     ]
     greet(at)
-    for load in incoming:
+    for load in incoming[:4]:
         load.start()
 
     device = lax.axis_index("seq") * depth + at.sub
     valid = kept_tokens(tok, device * tok, clip_ref, flags_ref)
+    valid_ref[...] = jnp.broadcast_to(valid, valid_ref.shape)
 
     def head(ref, h):
         return ref[h * E : (h + 1) * E, :]
@@ -225,6 +228,8 @@
     wide2[:, edge:] = jnp.zeros((wide2.shape[0], LANES), f32)
     for load in incoming[:4]:
         load.wait()
+    for load in incoming[4:]:
+        load.start()
     for h in range(H):
         feat, slope = key_parts(h)
         feat = feat.astype(bf16)
@@ -238,7 +243,7 @@
         row = lax.broadcasted_iota(jnp.int32, (E, E), 0)
         col = lax.broadcasted_iota(jnp.int32, (E, E), 1)
         for h in range(H):
-            spread = jnp.where(row == col, gain_ref[:, h * E : (h + 1) * E], 0.0)
+            spread = jnp.where(row == col, gain_ref[h * E : (h + 1) * E][None, :], 0.0)
             gain[h * E : (h + 1) * E, :] = jnp.sum(spread, axis=1, keepdims=True)
         for load in incoming[4:]:
             load.wait()
@@ -269,9 +274,6 @@
 
     velocity = dot(turned[...], normed[...], (1, 0))
     res_ref[...] = (velocity - teach[...].astype(f32)).astype(bf16)
-    res_out = pltpu.make_async_copy(res_ref, res_hbm, stores.at[0])
-    gq_out = pltpu.make_async_copy(gq_ref, gq_hbm, stores.at[1])
-    res_out.start()
     ngrad[...] = dot(weight[...], res_ref[...], (1, 0))
     for h in range(H):
         rows = slice(h * E, (h + 1) * E)
@@ -284,32 +286,27 @@
         for h in range(H):
             back = dot(square(wide1, h)[:E], head(ugrad, h), (0, 0))
             gq_ref[h * E : (h + 1) * E, :] = (query(h)[1] * back).astype(bf16)
-        gq_out.start()
 
     all_total(
         at, pieces[1], wide2, near2, sent2, out2, half2, mine2, parts2, sems[8:], None, query_grads
     )
 
     grad_ref[...] = wide2[...].astype(bf16)
-    res_out.wait()
-    gq_out.wait()
 
 
 def finish_kernel(
-    first_ref, k_hbm, v_hbm, res_hbm, gq_hbm, grad_ref, clip_ref, flags_ref,
+    k, v, res, gq, grad_ref, valid_ref,
     res_out, gq_out, gk_out, gv_out,
-    k, v, res, gq, gk, gv, loads, stores,
+    gk, gv, stores,
 ):
-    tok = k.shape[1]
-    pairs = [(k_hbm, k), (v_hbm, v), (res_hbm, res), (gq_hbm, gq)]
-    incoming = [pltpu.make_async_copy(*pair, loads.at[i]) for i, pair in enumerate(pairs)]
-    pairs = [(res, res_out), (gq, gq_out), (gk, gk_out), (gv, gv_out)]
-    outgoing = [pltpu.make_async_copy(*pair, stores.at[i]) for i, pair in enumerate(pairs)]
-    for load in incoming:
-        load.start()
-    valid = kept_tokens(tok, first_ref[0], clip_ref, flags_ref)
-    incoming[0].wait()
-    incoming[1].wait()
+    whole = [
+        pltpu.make_async_copy(src, dst, stores.at[2 * H + i])
+        for i, (src, dst) in enumerate([(res, res_out), (gq, gq_out)])
+    ]
+    for store in whole:
+        store.start()
+    valid = valid_ref[:1, :]
+    outgoing = []
     for h in range(H):
         rows = slice(h * E, (h + 1) * E)
         total = grad_ref[:, rows]
@@ -318,13 +315,12 @@
         feat = (jnp.maximum(keys, 0.0) * valid).astype(bf16)
         gk[rows, :] = (slope * dot(total, v[rows, :], (0, 0))).astype(bf16)
         gv[rows, :] = dot(total, feat, (1, 0)).astype(bf16)
-        if h == 1:
-            for load, store in zip(incoming[2:], outgoing[:2]):
-                load.wait()
-                store.start()
-    outgoing[2].start()
-    outgoing[3].start()
-    for store in outgoing:
+        for i, (src, dst) in enumerate([(gk, gk_out), (gv, gv_out)]):
+            outgoing.append(
+                pltpu.make_async_copy(src.at[rows], dst.at[rows], stores.at[2 * h + i])
+            )
+            outgoing[-1].start()
+    for store in whole + outgoing:
         store.wait()
 
 
@@ -358,17 +354,20 @@
         totals += [vmem(half, bf16)] * 3
     arrays = (query_rows, key_rows, value_rows, query_tangent, key_tangent, value_tangent)
     arrays = tuple(array.T for array in arrays + (teacher,)) + (out_weight,)
-    anywhere = pl.BlockSpec(memory_space=pl.ANY)
+    anywhere = pl.BlockSpec(memory_space=pltpu.HBM)
     in_vmem = pl.BlockSpec(memory_space=vmem)
     in_smem = pl.BlockSpec(memory_space=pltpu.SMEM)
     wide_t = jax.ShapeDtypeStruct((width, tok), bf16)
     res_t = jax.ShapeDtypeStruct(teacher.shape[::-1], bf16)
-    res, grad_query, grad = pl.pallas_call(
+    handed = [(res_t.shape, bf16), (wide_t.shape, bf16), ((E, padded), bf16)]
+    handed += [(wide_t.shape, bf16)] * 2 + [((8, tok), f32)]
+    held = sum(rows * cols * jnp.dtype(kind).itemsize for (rows, cols), kind in handed)
+    res, grad_query, grad, keys, values, valid = pl.pallas_call(
         functools.partial(step_kernel, chips, depth, pieces),
-        out_shape=(res_t, wide_t, jax.ShapeDtypeStruct((E, padded), bf16)),
+        out_shape=[vmem(*piece) for piece in handed],
         in_specs=[anywhere] * 8 + [in_vmem, in_smem, in_smem],
-        out_specs=[anywhere, anywhere, in_vmem],
-        scratch_shapes=[vmem(array.shape, array.dtype) for array in arrays]
+        out_specs=[in_vmem] * 6,
+        scratch_shapes=[vmem(arrays[i].shape, bf16) for i in (0, 3, 4, 5, 6, 7)]
         + [dma((8,))]
         + totals
         + [
@@ -379,24 +378,20 @@
             vmem((width, tok), bf16),
             vmem(out_weight.shape[::-1], bf16),
             vmem((width, 1), f32),
-            vmem(res_t.shape, bf16),
-            vmem((width, tok), bf16),
-            dma((2,)),
         ]
         + ([dma, dma] + [dma((chips,))] * 6) * 2,
-        compiler_params=pltpu.CompilerParams(collective_id=0, has_side_effects=True),
-    )(*arrays, norm_gain[None, :], clip_length, block_mask)
-    first = (lax.axis_index("seq") * depth + lax.axis_index("sub")) * tok
+        compiler_params=pltpu.CompilerParams(
+            collective_id=0, has_side_effects=True, vmem_limit_bytes=VMEM_BYTES - held
+        ),
+    )(*arrays, norm_gain, clip_length, block_mask)
     outs = pl.pallas_call(
         finish_kernel,
         out_shape=(res_t, wide_t, wide_t, wide_t),
-        in_specs=[in_smem] + [anywhere] * 4 + [in_vmem, in_smem, in_smem],
+        in_specs=[in_vmem] * 6,
         out_specs=[anywhere] * 4,
-        scratch_shapes=[vmem(wide_t.shape, bf16)] * 2
-        + [vmem(res_t.shape, bf16)]
-        + [vmem(wide_t.shape, bf16)] * 3
-        + [dma((4,)), dma((4,))],
-    )(first[None], arrays[1], arrays[2], res, grad_query, grad, clip_length, block_mask)
+        scratch_shapes=[vmem(wide_t.shape, bf16)] * 2 + [dma((2 * H + 2,))],
+        compiler_params=pltpu.CompilerParams(vmem_limit_bytes=FINISH_VMEM),
+    )(keys, values, res, grad_query, grad, valid)
     return tuple(out.T for out in outs)
 
 

time: 53.7 us -> 49.1 us (0.914)
  Pallas kernels: 50.9 us -> 47.6 us
  local copies, waits for them, and re-layouts: 1.29 us -> 0 us
    pallas_call x1, Pallas kernels: 4.28 us -> 1.75 us  [local(): pl.pallas_call(finish_kernel, out_shape=(res_t, wide_t, wide_t, wide_t),...]
    broadcast_in_dim x1 -> x0, local copies, waits for them, and re-layouts: 1.29 us -> none  [local(): norm_gain[None, :]]
    pallas_call x1, Pallas kernels: 46.6 us -> 45.9 us  [local(): pl.pallas_call(functools.partial(step_kernel, chips, depth, pieces), out_...]
where the time goes in v1:
time: 49.1 us; the launch traced here: 48.9 us
  Pallas kernels  47.6 us (97%)
  between operations  1.29 us (3%)
    pallas_call x1, Pallas kernels, local(): pl.pallas_call(functools.partial(step_kernel, chips, depth, pieces), out_...  45.9 us
    pallas_call x1, Pallas kernels, local(): pl.pallas_call(finish_kernel, out_shape=(res_t, wide_t, wide_t, wide_t),...  1.75 us

profile of v1, /device:TPU:0, one launch (start us, length us, event | category | flops | bytes accessed | tf_op | source)
XLA Modules:
  0.0 48.9 jit_solution(8850708195064453749)
XLA Ops:
  1.3 45.9 %shard_map.138 = (bf16[2240,256]{1,0:T(8,128)(2,1)S(1)}, bf16[1120,256]{1,0:T(8,128)(2,1)S(1)}, bf16[112,1152]{1,0:T(8,128)(2,1)S(1)}, bf16[1120,256]{1,0:T(8,12...) custom-call(bf16[1120,256]{1,0:T(8,128)(2,1)} %bitcast.12, bf16[1120,256]{1,0:T(8,128)(2,1)} %bitcast.13, ...), custom_call_target="tpu_custom_call" | custom-call | tf_op jit(solution)/shard_map/pallas_call | solution.py:365
  47.2 1.7 %shard_map.139 = (bf16[2240,256]{1,0:T(8,128)(2,1)}, bf16[1120,256]{1,0:T(8,128)(2,1)}, bf16[1120,256]{1,0:T(8,128)(2,1)}, bf16[1120,256]{1,0:T(8,128)(2,1)}) custom-call(bf16[1120,256]{1,0:T(8,128)(2,1)S(1)} %get-tuple-element.14.k, bf16[1120,256]{1,0:T(8,128)(2,1)S(1)} %get-tuple-element.15.v, bf16[2240,256]{1,0:T(8,128)(2,1)S(1)} %get-tuple-element.16.res, ...), custom_call_target="tpu_custom_call" | custom-call | tf_op jit(solution)/shard_map/pallas_call | solution.py:387

commit v2 on v1

v2 whole, which is shorter than its diff:
```python
import functools

import jax
import jax.numpy as jnp
from jax import lax
from jax.experimental import pallas as pl
from jax.experimental.pallas import tpu as pltpu
from jax.sharding import PartitionSpec as P

H = 10
E = 112
BLK = 64


MESH = pl.DeviceIdType.MESH
LANES = 128
VMEM_BYTES = 67043328
FINISH_VMEM = 16 << 20
f32 = jnp.float32
bf16 = jnp.bfloat16


def norm_back(unnorm, scale_inv, weighted):
    inner_mean = jnp.mean(unnorm * weighted, axis=0, keepdims=True)
    return scale_inv * weighted - unnorm * (scale_inv * scale_inv * scale_inv) * inner_mean


def dot(left, right, over):
    return lax.dot_general(left, right, ((over[:1], over[1:]), ((), ())), preferred_element_type=f32)


class Where:
    def __init__(self, chips, depth):
        seq = lax.axis_index("seq")
        self.sub = lax.axis_index("sub")
        self.depth = depth
        self.planes = chips // depth
        self.layers = depth // 2
        self.group = chips // 2
        self.core = lax.rem(seq, 2)
        self.column = seq // 2
        self.layer = lax.rem(self.sub, self.layers)
        self.spot = self.column * self.layers + self.layer
        self.partner = (seq + 1 - 2 * self.core, self.sub)
        self.opposite = (self.partner[0], lax.rem(self.sub + self.layers, depth))

    def peer(self, spot):
        base = self.sub - self.layer
        seq = (spot // self.layers) * 2 + 1 - self.core
        return seq, base + lax.rem(spot, self.layers)

    def each(self, body, near_first=False):
        levels = range(self.layers) if near_first else range(self.layers)[::-1]
        for level in levels:
            layer = lax.rem(self.layer + level, self.layers)

            @pl.loop(0 if level else 1, self.planes)
            def _(step):
                body(lax.rem(self.column + step, self.planes) * self.layers + layer)


def greet(at):
    barrier = pltpu.get_barrier_semaphore()

    def hello(device):
        pl.semaphore_signal(barrier, inc=1, device_id=device, device_id_type=MESH)

    hello(at.opposite)
    at.each(lambda spot: hello(at.peer(spot)))
    hello(at.partner)


class Total:
    def __init__(self, at, piece, wide, near, sent, out, half, mine, parts, cross, sems):
        self.at, self.piece, self.wide = at, piece, wide
        self.near, self.sent, self.out = near, sent, out
        self.half, self.mine, self.parts, self.cross, self.sems = half, mine, parts, cross, sems

    def copy(self, src, dst, send, recv, to):
        return pltpu.make_async_remote_copy(
            src_ref=src,
            dst_ref=dst,
            send_sem=send,
            recv_sem=recv,
            device_id=to,
            device_id_type=MESH,
        )

    def rows(self, spot, side=None):
        base = spot if side is None else side * self.at.group + spot
        return pl.ds(pl.multiple_of(base * self.piece, 16), self.piece)

    def swap(self):
        span = self.at.group * self.piece
        other = pl.ds(pl.multiple_of((1 - self.at.core) * span, 16), span)
        return self.copy(
            self.sent.at[other], self.half, self.sems[0], self.sems[1], self.at.partner
        )

    def scatter(self, spot, slot):
        return self.copy(
            self.mine.at[self.rows(spot)],
            self.parts.at[self.rows(slot)],
            self.sems[2].at[spot],
            self.sems[3].at[slot],
            self.at.peer(spot),
        )

    def exchange(self):
        return [
            self.copy(
                self.cross.at[2],
                self.cross.at[i],
                self.sems[4].at[i],
                self.sems[5].at[i],
                to,
            )
            for i, to in enumerate([self.at.partner, self.at.opposite])
        ]

    def gather(self, spot, slot, side):
        return self.copy(
            self.out.at[self.rows(slot, side)],
            self.out.at[self.rows(slot, side)],
            self.sems[6].at[spot],
            self.sems[7].at[slot],
            self.at.peer(spot),
        )

    def forward(self, spot, side):
        return self.copy(
            self.out.at[self.rows(spot, side)],
            self.out.at[self.rows(spot, side)],
            self.sems[8].at[spot],
            self.sems[9].at[spot],
            self.at.partner,
        )

    def clear_edge(self):
        edge = self.wide.shape[1] - LANES
        self.wide[:, edge:] = jnp.zeros((self.wide.shape[0], LANES), f32)

    def pack(self):
        size = self.wide.shape[0]
        blocks = self.wide.shape[1] // LANES
        for block in range(blocks):
            lanes = self.wide[:, block * LANES : (block + 1) * LANES]
            self.near[block * size : (block + 1) * size, :] = lanes
            self.sent[block * size : (block + 1) * size, :] = lanes.astype(bf16)
        used = size * blocks
        left = self.near.shape[0] - used
        if left:
            self.near[used:, :] = jnp.zeros((left, LANES), f32)
            self.sent[used:, :] = jnp.zeros((left, LANES), bf16)

    def spread(self):
        at = self.at

        def one(spot):
            own = self.near[self.rows(spot, at.core), :]
            both = own + self.half[self.rows(spot), :].astype(f32)
            self.mine[self.rows(spot), :] = both.astype(bf16)
            self.scatter(spot, at.spot).start()

        at.each(one)
        one(at.spot)

    def reduce(self):
        at = self.at

        def add(spot):
            self.scatter(spot, spot).wait_recv()
            self.near[: self.piece, :] += self.parts[self.rows(spot), :].astype(f32)

        self.scatter(at.spot, at.spot).wait_recv()
        self.near[: self.piece, :] = self.parts[self.rows(at.spot), :].astype(f32)
        at.each(add, near_first=True)
        self.cross[2] = self.near[: self.piece, :].astype(bf16)
        for copy in self.exchange()[::-1]:
            copy.start()

    def settle(self):
        at = self.at
        for copy in self.exchange():
            copy.wait_recv()
        both = self.cross[0].astype(f32) + self.cross[1].astype(f32)
        self.out[self.rows(at.spot, at.core), :] = both.astype(bf16)

        def one(spot):
            self.gather(spot, at.spot, at.core).start()

        at.each(one)
        one(at.spot)

    def relay(self):
        side = 1 - self.at.core

        def one(spot):
            self.gather(spot, spot, side).wait_recv()
            self.forward(spot, side).start()

        self.at.each(one, near_first=True)
        self.gather(self.at.spot, self.at.spot, side).wait_recv()

    def arrive(self):
        at = self.at
        at.each(lambda spot: self.forward(spot, at.core).wait_recv(), near_first=True)
        size = self.wide.shape[0]
        for block in range(self.wide.shape[1] // LANES):
            self.wide[:, block * LANES : (block + 1) * LANES] = self.out[
                block * size : (block + 1) * size, :
            ].astype(f32)

    def drain(self):
        at = self.at
        self.swap().wait_send()

        def one(spot):
            self.scatter(spot, at.spot).wait_send()
            self.gather(spot, at.spot, at.core).wait_send()

        def other(spot):
            one(spot)
            self.forward(spot, 1 - at.core).wait_send()

        at.each(other)
        one(at.spot)
        for copy in self.exchange():
            copy.wait_send()


def kept_tokens(tok, first, clip_ref, flags_ref):
    token = lax.broadcasted_iota(jnp.int32, (8, tok), 1)
    kept = jnp.zeros((8, tok), jnp.int32)
    for block in range(tok // BLK):
        inside = (token >= block * BLK) & (token < (block + 1) * BLK)
        kept = jnp.where(inside, flags_ref[block], kept)
    before = token + first < clip_ref[0]
    return jnp.where(before & (kept == 1), 1.0, 0.0).astype(f32)[:1]


def step_kernel(
    chips, depth, piece,
    q_hbm, k_hbm, v_hbm, qt_hbm, kt_hbm, vt_hbm, t_hbm, w_hbm, gain_hbm, clip_hbm, flags_hbm,
    res_ref, gq_ref, grad_ref, k, v, valid_ref,
    q, qt, kt, vt, teach, weight, gain_ref, clip_ref, flags_ref, loads,
    states, part, unnorm, scale, normed, ngrad, ugrad, turned, gain,
    *rest,
):
    at = Where(chips, depth)
    greet(at)
    tok = q.shape[1]
    pairs = [
        (k_hbm, k),
        (v_hbm, v),
        (clip_hbm, clip_ref),
        (flags_hbm, flags_ref),
        (kt_hbm, kt),
        (vt_hbm, vt),
        (w_hbm, weight),
        (q_hbm, q),
        (qt_hbm, qt),
        (gain_hbm, gain_ref),
        (t_hbm, teach),
    ]
    incoming = [pltpu.make_async_copy(*pair, loads.at[i]) for i, pair in enumerate(pairs)]
    for load in incoming[:6]:
        load.start()
    state, state_dot, state_grad = (
        Total(at, piece, *rest[8 * i : 8 * i + 8], rest[24 + 10 * i : 34 + 10 * i]) for i in range(3)
    )

    def head(ref, h):
        return ref[h * E : (h + 1) * E, :]

    def square(ref, h):
        return ref[:, h * E : (h + 1) * E].astype(bf16)

    def cols(h):
        return slice(h * E, (h + 1) * E)

    for total in (state, state_dot, state_grad):
        total.clear_edge()
    for load in incoming[:4]:
        load.wait()
    for load in incoming[6:]:
        load.start()
    device = lax.axis_index("seq") * depth + at.sub
    valid = kept_tokens(tok, device * tok, clip_ref, flags_ref)
    valid_ref[...] = jnp.broadcast_to(valid, valid_ref.shape)
    for h in range(H):
        feat = (jnp.maximum(head(k, h).astype(f32), 0.0) * valid).astype(bf16)
        ugrad[cols(h), :] = feat
        state.wide[:, cols(h)] = dot(head(v, h), feat, (1, 1))
    state.pack()
    pl.semaphore_wait(pltpu.get_barrier_semaphore(), at.group + 1)
    state.swap().start()
    for load in incoming[4:6]:
        load.wait()
    for h in range(H):
        slope = jnp.where(head(k, h).astype(f32) > 0, 1.0, 0.0) * valid
        along = (slope * head(kt, h).astype(f32)).astype(bf16)
        state_dot.wide[:, cols(h)] = dot(head(v, h), along, (1, 1)) + dot(
            head(vt, h), head(ugrad, h), (1, 1)
        )
    state_dot.pack()
    state_dot.swap().start()
    state.swap().wait_recv()
    state.spread()
    state_dot.swap().wait_recv()
    state_dot.spread()

    for load in incoming[6:]:
        load.wait()
    row = lax.broadcasted_iota(jnp.int32, (E, E), 0)
    col = lax.broadcasted_iota(jnp.int32, (E, E), 1)
    for h in range(H):
        spread = jnp.where(row == col, gain_ref[cols(h)][None, :], 0.0)
        gain[cols(h), :] = jnp.sum(spread, axis=1, keepdims=True)
    for start in range(0, weight.shape[1], 256):
        stop = min(start + 256, weight.shape[1])
        turned[start:stop, :] = weight[:, start:stop].T

    state.reduce()
    state_dot.reduce()
    state.settle()
    state_dot.settle()

    def query(h):
        rows = head(q, h).astype(f32)
        return jnp.maximum(rows, 0.0).astype(bf16), jnp.where(rows > 0, 1.0, 0.0).astype(f32)

    state.relay()
    state.arrive()
    for h in range(H):
        feat, slope = query(h)
        along = (slope * head(qt, h).astype(f32)).astype(bf16)
        matrix = square(state.wide, h)
        states[h] = matrix
        un = dot(matrix, feat, (1, 0))
        unnorm[cols(h), :] = un
        scale[h] = lax.rsqrt(jnp.mean(un * un, axis=0, keepdims=True) + 1e-06)
        part[cols(h), :] = dot(matrix, along, (1, 0))
    state_dot.relay()
    state_dot.arrive()
    for h in range(H):
        un_dot = head(part, h) + dot(square(state_dot.wide, h), query(h)[0], (1, 0))
        back = norm_back(head(unnorm, h), scale[h], un_dot)
        normed[cols(h), :] = (gain[cols(h), :] * back).astype(bf16)

    velocity = dot(turned[...], normed[...], (1, 0))
    res_ref[...] = (velocity - teach[...].astype(f32)).astype(bf16)
    ngrad[...] = dot(weight[...], res_ref[...], (1, 0))
    for h in range(H):
        weighted = gain[cols(h), :] * head(ngrad, h)
        grad = norm_back(head(unnorm, h), scale[h], weighted).astype(bf16)
        ugrad[cols(h), :] = grad
        state_grad.wide[:, cols(h)] = dot(grad, query(h)[0], (1, 1))
    state_grad.pack()
    state_grad.swap().start()
    state_grad.swap().wait_recv()
    state_grad.spread()
    for h in range(H):
        back = dot(states[h], head(ugrad, h), (0, 0))
        gq_ref[cols(h), :] = (query(h)[1] * back).astype(bf16)
    state.drain()
    state_dot.drain()
    state_grad.reduce()
    state_grad.settle()
    state_grad.relay()
    state_grad.arrive()
    grad_ref[...] = state_grad.wide[...].astype(bf16)
    state_grad.drain()


def finish_kernel(
    k, v, res, gq, grad_ref, valid_ref,
    res_out, gq_out, gk_out, gv_out,
    gk, gv, stores,
):
    whole = [
        pltpu.make_async_copy(src, dst, stores.at[2 * H + i])
        for i, (src, dst) in enumerate([(res, res_out), (gq, gq_out)])
    ]
    for store in whole:
        store.start()
    valid = valid_ref[:1, :]
    outgoing = []
    for h in range(H):
        rows = slice(h * E, (h + 1) * E)
        total = grad_ref[:, rows]
        keys = k[rows, :].astype(f32)
        slope = jnp.where(keys > 0, 1.0, 0.0) * valid
        feat = (jnp.maximum(keys, 0.0) * valid).astype(bf16)
        gk[rows, :] = (slope * dot(total, v[rows, :], (0, 0))).astype(bf16)
        gv[rows, :] = dot(total, feat, (1, 0)).astype(bf16)
        for i, (src, dst) in enumerate([(gk, gk_out), (gv, gv_out)]):
            outgoing.append(
                pltpu.make_async_copy(src.at[rows], dst.at[rows], stores.at[2 * h + i])
            )
            outgoing[-1].start()
    for store in whole + outgoing:
        store.wait()


def local(
    query_rows,
    key_rows,
    value_rows,
    query_tangent,
    key_tangent,
    value_tangent,
    teacher,
    out_weight,
    norm_gain,
    clip_length,
    block_mask,
):
    tok, width = query_rows.shape
    depth = lax.axis_size("sub")
    chips = lax.axis_size("seq") // 2 * depth
    padded = -(-width // LANES) * LANES
    vmem = pltpu.VMEM
    dma = pltpu.SemaphoreType.DMA
    group = chips // 2
    piece = -(-(E * padded // LANES) // (32 * group)) * 16
    half = (group * piece, LANES)
    full = (2 * group * piece, LANES)
    total = [vmem((E, padded), f32), vmem(full, f32), vmem(full, bf16), vmem(full, bf16)]
    total += [vmem(half, bf16)] * 3 + [vmem((3, piece, LANES), bf16)]
    arrays = (query_rows, key_rows, value_rows, query_tangent, key_tangent, value_tangent)
    arrays = tuple(array.T for array in arrays + (teacher,)) + (out_weight,)
    anywhere = pl.BlockSpec(memory_space=pltpu.HBM)
    in_vmem = pl.BlockSpec(memory_space=vmem)
    wide_t = jax.ShapeDtypeStruct((width, tok), bf16)
    res_t = jax.ShapeDtypeStruct(teacher.shape[::-1], bf16)
    handed = [(res_t.shape, bf16), (wide_t.shape, bf16), ((E, padded), bf16)]
    handed += [(wide_t.shape, bf16)] * 2 + [((8, tok), f32)]
    held = sum(rows * cols * jnp.dtype(kind).itemsize for (rows, cols), kind in handed)
    res, grad_query, grad, keys, values, valid = pl.pallas_call(
        functools.partial(step_kernel, chips, depth, piece),
        out_shape=[vmem(*piece) for piece in handed],
        in_specs=[anywhere] * 11,
        out_specs=[in_vmem] * 6,
        scratch_shapes=[vmem(arrays[i].shape, bf16) for i in (0, 3, 4, 5, 6, 7)]
        + [vmem(norm_gain.shape, f32)]
        + [pltpu.SMEM(array.shape, jnp.int32) for array in (clip_length, block_mask)]
        + [dma((11,))]
        + [
            vmem((H, E, E), bf16),
            vmem((width, tok), f32),
            vmem((width, tok), f32),
            vmem((H, 1, tok), f32),
            vmem((width, tok), bf16),
            vmem((width, tok), f32),
            vmem((width, tok), bf16),
            vmem(out_weight.shape[::-1], bf16),
            vmem((width, 1), f32),
        ]
        + total * 3
        + ([dma, dma] + [dma((group,))] * 2 + [dma((2,))] * 2 + [dma((group,))] * 4) * 3,
        compiler_params=pltpu.CompilerParams(
            collective_id=0, has_side_effects=True, vmem_limit_bytes=VMEM_BYTES - held
        ),
    )(*arrays, norm_gain, clip_length, block_mask)
    outs = pl.pallas_call(
        finish_kernel,
        out_shape=(res_t, wide_t, wide_t, wide_t),
        in_specs=[in_vmem] * 6,
        out_specs=[anywhere] * 4,
        scratch_shapes=[vmem(wide_t.shape, bf16)] * 2 + [dma((2 * H + 2,))],
        compiler_params=pltpu.CompilerParams(vmem_limit_bytes=FINISH_VMEM),
    )(keys, values, res, grad_query, grad, valid)
    return tuple(out.T for out in outs)


def solution(mesh):
    return jax.shard_map(
        local,
        mesh=mesh,
        in_specs=(
            P(("seq", "sub"), None),
            P(("seq", "sub"), None),
            P(("seq", "sub"), None),
            P(("seq", "sub"), None),
            P(("seq", "sub"), None),
            P(("seq", "sub"), None),
            P(("seq", "sub"), None),
            P(),
            P(),
            P(),
            P(("seq", "sub")),
        ),
        out_specs=(
            P(("seq", "sub"), None),
            P(("seq", "sub"), None),
            P(("seq", "sub"), None),
            P(("seq", "sub"), None),
        ),
        check_vma=False,
    )
```

time: 49.1 us -> 43.3 us (0.88)
  Pallas kernels: 47.6 us -> 41.8 us
    pallas_call x1, Pallas kernels: 45.9 us -> 40.1 us  [local(): pl.pallas_call(functools.partial(step_kernel, chips, depth, piece), out_s...]
where the time goes in v2:
time: 43.3 us; the launch traced here: 43.1 us
  Pallas kernels  41.8 us (97%)
  between operations  1.29 us (3%)
    pallas_call x1, Pallas kernels, local(): pl.pallas_call(functools.partial(step_kernel, chips, depth, piece), out_s...  40.1 us
    pallas_call x1, Pallas kernels, local(): pl.pallas_call(finish_kernel, out_shape=(res_t, wide_t, wide_t, wide_t),...  1.75 us

profile of v2, /device:TPU:0, one launch (start us, length us, event | category | flops | bytes accessed | tf_op | source)
XLA Modules:
  0.0 43.1 jit_solution(17184490236402265624)
XLA Ops:
  1.3 40.1 %shard_map.138 = (bf16[2240,256]{1,0:T(8,128)(2,1)S(1)}, bf16[1120,256]{1,0:T(8,128)(2,1)S(1)}, bf16[112,1152]{1,0:T(8,128)(2,1)S(1)}, bf16[1120,256]{1,0:T(8,12...) custom-call(bf16[1120,256]{1,0:T(8,128)(2,1)} %bitcast.12, bf16[1120,256]{1,0:T(8,128)(2,1)} %bitcast.13, ...), custom_call_target="tpu_custom_call" | custom-call | tf_op jit(solution)/shard_map/pallas_call | solution.py:440
  41.4 1.7 %shard_map.139 = (bf16[2240,256]{1,0:T(8,128)(2,1)}, bf16[1120,256]{1,0:T(8,128)(2,1)}, bf16[1120,256]{1,0:T(8,128)(2,1)}, bf16[1120,256]{1,0:T(8,128)(2,1)}) custom-call(bf16[1120,256]{1,0:T(8,128)(2,1)S(1)} %get-tuple-element.14.k, bf16[1120,256]{1,0:T(8,128)(2,1)S(1)} %get-tuple-element.15.v, bf16[2240,256]{1,0:T(8,128)(2,1)S(1)} %get-tuple-element.16.res, ...), custom_call_target="tpu_custom_call" | custom-call | tf_op jit(solution)/shard_map/pallas_call | solution.py:466

commit v3 on v2

--- a/solution.py
+++ b/solution.py
@@ -71,8 +71,9 @@
 
 
 class Total:
-    def __init__(self, at, piece, wide, near, sent, out, half, mine, parts, cross, sems):
-        self.at, self.piece, self.wide = at, piece, wide
+    def __init__(self, at, blocks, wide, near, sent, out, half, mine, parts, cross, sems):
+        self.at, self.blocks, self.wide = at, blocks, wide
+        self.piece = cross.shape[1]
         self.near, self.sent, self.out = near, sent, out
         self.half, self.mine, self.parts, self.cross, self.sems = half, mine, parts, cross, sems
 
@@ -136,18 +137,20 @@
             self.at.partner,
         )
 
-    def clear_edge(self):
-        edge = self.wide.shape[1] - LANES
-        self.wide[:, edge:] = jnp.zeros((self.wide.shape[0], LANES), f32)
+    def views(self):
+        size = self.wide.shape[0]
+        for step, block in enumerate(self.blocks):
+            yield (
+                slice(block * LANES, (block + 1) * LANES),
+                slice(step * size, (step + 1) * size),
+            )
 
     def pack(self):
-        size = self.wide.shape[0]
-        blocks = self.wide.shape[1] // LANES
-        for block in range(blocks):
-            lanes = self.wide[:, block * LANES : (block + 1) * LANES]
-            self.near[block * size : (block + 1) * size, :] = lanes
-            self.sent[block * size : (block + 1) * size, :] = lanes.astype(bf16)
-        used = size * blocks
+        for cols, rows in self.views():
+            lanes = self.wide[:, cols]
+            self.near[rows, :] = lanes
+            self.sent[rows, :] = lanes.astype(bf16)
+        used = self.wide.shape[0] * len(self.blocks)
         left = self.near.shape[0] - used
         if left:
             self.near[used:, :] = jnp.zeros((left, LANES), f32)
@@ -202,14 +205,11 @@
         self.at.each(one, near_first=True)
         self.gather(self.at.spot, self.at.spot, side).wait_recv()
 
-    def arrive(self):
+    def arrive(self, result):
         at = self.at
         at.each(lambda spot: self.forward(spot, at.core).wait_recv(), near_first=True)
-        size = self.wide.shape[0]
-        for block in range(self.wide.shape[1] // LANES):
-            self.wide[:, block * LANES : (block + 1) * LANES] = self.out[
-                block * size : (block + 1) * size, :
-            ].astype(f32)
+        for cols, rows in self.views():
+            result[:, cols] = self.out[rows, :].astype(result.dtype)
 
     def drain(self):
         at = self.at
@@ -240,7 +240,7 @@
 
 
 def step_kernel(
-    chips, depth, piece,
+    chips, depth, spans,
     q_hbm, k_hbm, v_hbm, qt_hbm, kt_hbm, vt_hbm, t_hbm, w_hbm, gain_hbm, clip_hbm, flags_hbm,
     res_ref, gq_ref, grad_ref, k, v, valid_ref,
     q, qt, kt, vt, teach, weight, gain_ref, clip_ref, flags_ref, loads,
@@ -266,9 +266,15 @@
     incoming = [pltpu.make_async_copy(*pair, loads.at[i]) for i, pair in enumerate(pairs)]
     for load in incoming[:6]:
         load.start()
-    state, state_dot, state_grad = (
-        Total(at, piece, *rest[8 * i : 8 * i + 8], rest[24 + 10 * i : 34 + 10 * i]) for i in range(3)
+    wides = rest[:3]
+    bufs, sems = rest[3 : 3 + 7 * len(spans)], rest[3 + 7 * len(spans) :]
+    state, state_dot, early, late = (
+        Total(
+            at, span, wides[min(i, 2)], *bufs[7 * i : 7 * i + 7], sems[10 * i : 10 * i + 10]
+        )
+        for i, span in enumerate(spans)
     )
+    lead = -(-len(early.blocks) * LANES // E)
 
     def head(ref, h):
         return ref[h * E : (h + 1) * E, :]
@@ -279,8 +285,9 @@
     def cols(h):
         return slice(h * E, (h + 1) * E)
 
-    for total in (state, state_dot, state_grad):
-        total.clear_edge()
+    for wide in wides:
+        edge = wide.shape[1] - LANES
+        wide[:, edge:] = jnp.zeros((wide.shape[0], LANES), f32)
     for load in incoming[:4]:
         load.wait()
     for load in incoming[6:]:
@@ -331,7 +338,8 @@
         return jnp.maximum(rows, 0.0).astype(bf16), jnp.where(rows > 0, 1.0, 0.0).astype(f32)
 
     state.relay()
-    state.arrive()
+    state_dot.relay()
+    state.arrive(state.wide)
     for h in range(H):
         feat, slope = query(h)
         along = (slope * head(qt, h).astype(f32)).astype(bf16)
@@ -341,8 +349,7 @@
         unnorm[cols(h), :] = un
         scale[h] = lax.rsqrt(jnp.mean(un * un, axis=0, keepdims=True) + 1e-06)
         part[cols(h), :] = dot(matrix, along, (1, 0))
-    state_dot.relay()
-    state_dot.arrive()
+    state_dot.arrive(state_dot.wide)
     for h in range(H):
         un_dot = head(part, h) + dot(square(state_dot.wide, h), query(h)[0], (1, 0))
         back = norm_back(head(unnorm, h), scale[h], un_dot)
@@ -350,27 +357,41 @@
 
     velocity = dot(turned[...], normed[...], (1, 0))
     res_ref[...] = (velocity - teach[...].astype(f32)).astype(bf16)
-    ngrad[...] = dot(weight[...], res_ref[...], (1, 0))
-    for h in range(H):
-        weighted = gain[cols(h), :] * head(ngrad, h)
-        grad = norm_back(head(unnorm, h), scale[h], weighted).astype(bf16)
-        ugrad[cols(h), :] = grad
-        state_grad.wide[:, cols(h)] = dot(grad, query(h)[0], (1, 1))
-    state_grad.pack()
-    state_grad.swap().start()
-    state_grad.swap().wait_recv()
-    state_grad.spread()
+
+    def grads(first, last):
+        rows = slice(first * E, last * E)
+        ngrad[rows, :] = dot(weight[rows, :], res_ref[...], (1, 0))
+        for h in range(first, last):
+            weighted = gain[cols(h), :] * head(ngrad, h)
+            grad = norm_back(head(unnorm, h), scale[h], weighted).astype(bf16)
+            ugrad[cols(h), :] = grad
+            early.wide[:, cols(h)] = dot(grad, query(h)[0], (1, 1))
+
+    grads(0, lead)
+    early.pack()
+    early.swap().start()
+    grads(lead, H)
+    late.pack()
+    late.swap().start()
+    early.swap().wait_recv()
+    early.spread()
+    late.swap().wait_recv()
+    late.spread()
     for h in range(H):
         back = dot(states[h], head(ugrad, h), (0, 0))
         gq_ref[cols(h), :] = (query(h)[1] * back).astype(bf16)
     state.drain()
     state_dot.drain()
-    state_grad.reduce()
-    state_grad.settle()
-    state_grad.relay()
-    state_grad.arrive()
-    grad_ref[...] = state_grad.wide[...].astype(bf16)
-    state_grad.drain()
+    early.reduce()
+    late.reduce()
+    early.settle()
+    late.settle()
+    early.relay()
+    late.relay()
+    early.arrive(grad_ref)
+    late.arrive(grad_ref)
+    early.drain()
+    late.drain()
 
 
 def finish_kernel(
@@ -423,11 +444,17 @@
     vmem = pltpu.VMEM
     dma = pltpu.SemaphoreType.DMA
     group = chips // 2
-    piece = -(-(E * padded // LANES) // (32 * group)) * 16
-    half = (group * piece, LANES)
-    full = (2 * group * piece, LANES)
-    total = [vmem((E, padded), f32), vmem(full, f32), vmem(full, bf16), vmem(full, bf16)]
-    total += [vmem(half, bf16)] * 3 + [vmem((3, piece, LANES), bf16)]
+    group = chips // 2
+    blocks = padded // LANES
+    cut = -(-blocks // 2)
+    spans = [range(blocks)] * 2 + [range(cut), range(cut, blocks)]
+    totals = [vmem((E, padded), f32)] * 3
+    for span in spans:
+        piece = -(-(E * len(span)) // (32 * group)) * 16
+        half = (group * piece, LANES)
+        full = (2 * group * piece, LANES)
+        totals += [vmem(full, f32), vmem(full, bf16), vmem(full, bf16)]
+        totals += [vmem(half, bf16)] * 3 + [vmem((3, piece, LANES), bf16)]
     arrays = (query_rows, key_rows, value_rows, query_tangent, key_tangent, value_tangent)
     arrays = tuple(array.T for array in arrays + (teacher,)) + (out_weight,)
     anywhere = pl.BlockSpec(memory_space=pltpu.HBM)
@@ -438,7 +465,7 @@
     handed += [(wide_t.shape, bf16)] * 2 + [((8, tok), f32)]
     held = sum(rows * cols * jnp.dtype(kind).itemsize for (rows, cols), kind in handed)
     res, grad_query, grad, keys, values, valid = pl.pallas_call(
-        functools.partial(step_kernel, chips, depth, piece),
+        functools.partial(step_kernel, chips, depth, spans),
         out_shape=[vmem(*piece) for piece in handed],
         in_specs=[anywhere] * 11,
         out_specs=[in_vmem] * 6,
@@ -457,8 +484,8 @@
             vmem(out_weight.shape[::-1], bf16),
             vmem((width, 1), f32),
         ]
-        + total * 3
-        + ([dma, dma] + [dma((group,))] * 2 + [dma((2,))] * 2 + [dma((group,))] * 4) * 3,
+        + totals
+        + ([dma, dma] + [dma((group,))] * 2 + [dma((2,))] * 2 + [dma((group,))] * 4) * len(spans),
         compiler_params=pltpu.CompilerParams(
             collective_id=0, has_side_effects=True, vmem_limit_bytes=VMEM_BYTES - held
         ),

time: 43.3 us -> 42.6 us (0.984)
  Pallas kernels: 41.8 us -> 41.2 us
    pallas_call x1, Pallas kernels: 40.1 us -> 39.4 us  [local(): pl.pallas_call(functools.partial(step_kernel, chips, depth, spans), out_s...]
where the time goes in v3:
time: 42.6 us; the launch traced here: 42.5 us
  Pallas kernels  41.2 us (97%)
  between operations  1.29 us (3%)
    pallas_call x1, Pallas kernels, local(): pl.pallas_call(functools.partial(step_kernel, chips, depth, spans), out_s...  39.4 us
    pallas_call x1, Pallas kernels, local(): pl.pallas_call(finish_kernel, out_shape=(res_t, wide_t, wide_t, wide_t),...  1.75 us

profile of v3, /device:TPU:0, one launch (start us, length us, event | category | flops | bytes accessed | tf_op | source)
XLA Modules:
  0.0 42.5 jit_solution(14611372030468677186)
XLA Ops:
  1.3 39.4 %shard_map.138 = (bf16[2240,256]{1,0:T(8,128)(2,1)S(1)}, bf16[1120,256]{1,0:T(8,128)(2,1)S(1)}, bf16[112,1152]{1,0:T(8,128)(2,1)S(1)}, bf16[1120,256]{1,0:T(8,12...) custom-call(bf16[1120,256]{1,0:T(8,128)(2,1)} %bitcast.12, bf16[1120,256]{1,0:T(8,128)(2,1)} %bitcast.13, ...), custom_call_target="tpu_custom_call" | custom-call | tf_op jit(solution)/shard_map/pallas_call | solution.py:467
  40.7 1.7 %shard_map.139 = (bf16[2240,256]{1,0:T(8,128)(2,1)}, bf16[1120,256]{1,0:T(8,128)(2,1)}, bf16[1120,256]{1,0:T(8,128)(2,1)}, bf16[1120,256]{1,0:T(8,128)(2,1)}) custom-call(bf16[1120,256]{1,0:T(8,128)(2,1)S(1)} %get-tuple-element.14.k, bf16[1120,256]{1,0:T(8,128)(2,1)S(1)} %get-tuple-element.15.v, bf16[2240,256]{1,0:T(8,128)(2,1)S(1)} %get-tuple-element.16.res, ...), custom_call_target="tpu_custom_call" | custom-call | tf_op jit(solution)/shard_map/pallas_call | solution.py:493

commit v4 on v3

--- a/solution.py
+++ b/solution.py
@@ -244,7 +244,7 @@
     q_hbm, k_hbm, v_hbm, qt_hbm, kt_hbm, vt_hbm, t_hbm, w_hbm, gain_hbm, clip_hbm, flags_hbm,
     res_ref, gq_ref, grad_ref, k, v, valid_ref,
     q, qt, kt, vt, teach, weight, gain_ref, clip_ref, flags_ref, loads,
-    states, part, unnorm, scale, normed, ngrad, ugrad, turned, gain,
+    flat, flat_dot, part, unnorm, scale, normed, ngrad, ugrad, turned, gain,
     *rest,
 ):
     at = Where(chips, depth)
@@ -279,9 +279,6 @@
     def head(ref, h):
         return ref[h * E : (h + 1) * E, :]
 
-    def square(ref, h):
-        return ref[:, h * E : (h + 1) * E].astype(bf16)
-
     def cols(h):
         return slice(h * E, (h + 1) * E)
 
@@ -339,19 +336,18 @@
 
     state.relay()
     state_dot.relay()
-    state.arrive(state.wide)
+    state.arrive(flat)
     for h in range(H):
         feat, slope = query(h)
         along = (slope * head(qt, h).astype(f32)).astype(bf16)
-        matrix = square(state.wide, h)
-        states[h] = matrix
+        matrix = flat[:, cols(h)]
         un = dot(matrix, feat, (1, 0))
         unnorm[cols(h), :] = un
         scale[h] = lax.rsqrt(jnp.mean(un * un, axis=0, keepdims=True) + 1e-06)
         part[cols(h), :] = dot(matrix, along, (1, 0))
-    state_dot.arrive(state_dot.wide)
-    for h in range(H):
-        un_dot = head(part, h) + dot(square(state_dot.wide, h), query(h)[0], (1, 0))
+    state_dot.arrive(flat_dot)
+    for h in range(H):
+        un_dot = head(part, h) + dot(flat_dot[:, cols(h)], query(h)[0], (1, 0))
         back = norm_back(head(unnorm, h), scale[h], un_dot)
         normed[cols(h), :] = (gain[cols(h), :] * back).astype(bf16)
 
@@ -378,7 +374,7 @@
     late.swap().wait_recv()
     late.spread()
     for h in range(H):
-        back = dot(states[h], head(ugrad, h), (0, 0))
+        back = dot(flat[:, cols(h)], head(ugrad, h), (0, 0))
         gq_ref[cols(h), :] = (query(h)[1] * back).astype(bf16)
     state.drain()
     state_dot.drain()
@@ -474,7 +470,8 @@
         + [pltpu.SMEM(array.shape, jnp.int32) for array in (clip_length, block_mask)]
         + [dma((11,))]
         + [
-            vmem((H, E, E), bf16),
+            vmem((E, padded), bf16),
+            vmem((E, padded), bf16),
             vmem((width, tok), f32),
             vmem((width, tok), f32),
             vmem((H, 1, tok), f32),

time: 42.6 us -> 42.7 us (level)
  no operation moved by 1% of the time
where the time goes in v4:
time: 42.7 us; the launch traced here: 42.5 us
  Pallas kernels  41.2 us (96%)
  between operations  1.29 us (3%)
    pallas_call x1, Pallas kernels, local(): pl.pallas_call(functools.partial(step_kernel, chips, depth, spans), out_s...  39.5 us
    pallas_call x1, Pallas kernels, local(): pl.pallas_call(finish_kernel, out_shape=(res_t, wide_t, wide_t, wide_t),...  1.75 us

profile of v4, /device:TPU:0, one launch (start us, length us, event | category | flops | bytes accessed | tf_op | source)
XLA Modules:
  0.0 42.5 jit_solution(9522016635647050656)
XLA Ops:
  1.3 39.5 %shard_map.138 = (bf16[2240,256]{1,0:T(8,128)(2,1)S(1)}, bf16[1120,256]{1,0:T(8,128)(2,1)S(1)}, bf16[112,1152]{1,0:T(8,128)(2,1)S(1)}, bf16[1120,256]{1,0:T(8,12...) custom-call(bf16[1120,256]{1,0:T(8,128)(2,1)} %bitcast.12, bf16[1120,256]{1,0:T(8,128)(2,1)} %bitcast.13, ...), custom_call_target="tpu_custom_call" | custom-call | tf_op jit(solution)/shard_map/pallas_call | solution.py:463
  40.8 1.7 %shard_map.139 = (bf16[2240,256]{1,0:T(8,128)(2,1)}, bf16[1120,256]{1,0:T(8,128)(2,1)}, bf16[1120,256]{1,0:T(8,128)(2,1)}, bf16[1120,256]{1,0:T(8,128)(2,1)}) custom-call(bf16[1120,256]{1,0:T(8,128)(2,1)S(1)} %get-tuple-element.14.k, bf16[1120,256]{1,0:T(8,128)(2,1)S(1)} %get-tuple-element.15.v, bf16[2240,256]{1,0:T(8,128)(2,1)S(1)} %get-tuple-element.16.res, ...), custom_call_target="tpu_custom_call" | custom-call | tf_op jit(solution)/shard_map/pallas_call | solution.py:490
